TPU v7x, 32 devices: a whole 2x2x4 slice. The times are simulated.
32 devices in a mesh: groups: 2 (over y), dp: 4 (over x, core), tensor: 4 (over z).
Axes of the slice: x: 2, y: 2, z: 4, core: 2. Of those that a mesh axis runs over, the one named last changes fastest.
Arguments:
- query: bfloat16 [4096, 512], P(('groups', 'dp'), 'tensor'), parts along dimension 0, may hold values from -4.5 to 4.5
- keys: bfloat16 [4096, 512], P(('groups', 'dp'), 'tensor'), parts along dimension 0, may hold values from -4.5 to 4.5
- values: bfloat16 [4096, 512], P(('groups', 'dp'), 'tensor'), parts along dimension 0, may hold values from -6 to 6
- upstream: bfloat16 [4096, 8192], P(('groups', 'dp', 'tensor')), parts along dimension 0, may hold values from -6 to 6
- projection: bfloat16 [512, 8192], P('tensor', 'dp'), may hold values from -0.0625 to 0.0625
- lengths: int32 [8, 8], P(('groups', 'dp')), parts along dimension 0, may hold values from 1 to 256, 512 in all within a row
Outputs:
- grad_query: bfloat16 [4096, 512], P(('groups', 'dp'), 'tensor'), parts along dimension 0
- grad_keys: bfloat16 [4096, 512], P(('groups', 'dp'), 'tensor'), parts along dimension 0
- grad_values: bfloat16 [4096, 512], P(('groups', 'dp'), 'tensor'), parts along dimension 0
- grad_projection: float32 [1024, 8192], P(('groups', 'tensor'), 'dp'), parts along dimension 0
There are 2 independent parts, one for each index of `groups`. A program takes and returns all parts, laid end to end along the dimension named above; an argument that names none is the same for every part. Nothing has to cross between parts.
Inputs may be any that keep to these rules, and one draw needn't show every extreme that they name: Each row holds the lengths of the 8 documents of one sequence in order; they sum to 512 and the largest is exactly 256.
All inputs are finite; a program needn't handle non-finite values.
Results may differ from a plain program's by a relative error of at most 0.014.
Values may be sent and summed in bfloat16 or wider, within the bound.
No kernel may reach another device: no remote copies, remote signals or barrier semaphores. Data moves between devices by JAX's collectives and lax.ppermute only.
A program may use at most 64 MiB of HBM per device.

v0:
```python
import jax
import jax.numpy as jnp
from jax import lax
from jax.sharding import PartitionSpec as P

HD = 128


def sequence_mask(length_row, row_count):
    segment_ends = jnp.cumsum(length_row)
    places = jnp.arange(row_count, dtype=jnp.int32)
    labels = jnp.sum((segment_ends[None, :] <= places[:, None]).astype(jnp.int32), axis=1)
    same = labels[:, None] == labels[None, :]
    return jnp.logical_and(same, places[None, :] <= places[:, None])


def shards(query, keys, values, upstream, projection, lengths):
    row_count, width = query.shape
    head_count = width // HD
    scaling = HD ** (-0.5)
    allowed = sequence_mask(lengths[0], row_count)
    query_heads = query.reshape(row_count, head_count, HD)
    key_heads = keys.reshape(row_count, head_count, HD)
    value_heads = values.reshape(row_count, head_count, HD)
    scores = (
        jnp.einsum("qhd,khd->hqk", query_heads, key_heads, preferred_element_type=jnp.float32)
        * scaling
    )
    scores = jnp.where(allowed[None], scores, -1e30)
    row_max = jnp.max(scores, axis=2, keepdims=True)
    exponent = jnp.exp(scores - row_max)
    probs = exponent / jnp.sum(exponent, axis=2, keepdims=True)
    probs_low = probs.astype(jnp.bfloat16)
    attended = jnp.einsum(
        "hqk,khd->qhd", probs_low, value_heads, preferred_element_type=jnp.float32
    )
    attended = attended.astype(jnp.bfloat16).reshape(row_count, width)
    full_projection = lax.all_gather(projection, "dp", axis=1, tiled=True)
    gathered = lax.all_gather(upstream, "tensor", axis=0, tiled=True)
    out_total = lax.dot_general(
        gathered, full_projection, (((1,), (1,)), ((), ())), preferred_element_type=jnp.float32
    )
    partial_grad = lax.dot_general(
        attended, gathered, (((0,), (0,)), ((), ())), preferred_element_type=jnp.float32
    )
    grad_projection = lax.psum_scatter(
        partial_grad.astype(jnp.bfloat16), "dp", scatter_dimension=1, tiled=True
    ).astype(jnp.float32)
    out_grad = out_total.astype(jnp.bfloat16)
    grad_heads = out_grad.reshape(row_count, head_count, HD)
    grad_values = jnp.einsum(
        "hqk,qhd->khd", probs_low, grad_heads, preferred_element_type=jnp.float32
    ).astype(jnp.bfloat16)
    grad_probs = jnp.einsum(
        "qhd,khd->hqk", grad_heads, value_heads, preferred_element_type=jnp.float32
    )
    delta = jnp.sum(probs * grad_probs, axis=2, keepdims=True)
    grad_scores = (probs * (grad_probs - delta) * scaling).astype(jnp.bfloat16)
    grad_query = jnp.einsum(
        "hqk,khd->qhd", grad_scores, key_heads, preferred_element_type=jnp.float32
    ).astype(jnp.bfloat16)
    grad_keys = jnp.einsum(
        "hqk,qhd->khd", grad_scores, query_heads, preferred_element_type=jnp.float32
    ).astype(jnp.bfloat16)
    return (
        grad_query.reshape(row_count, width),
        grad_keys.reshape(row_count, width),
        grad_values.reshape(row_count, width),
        grad_projection,
    )


def solution(mesh):
    in_specs = (
        P(("groups", "dp"), "tensor"),
        P(("groups", "dp"), "tensor"),
        P(("groups", "dp"), "tensor"),
        P(("groups", "dp", "tensor"), None),
        P("tensor", "dp"),
        P(("groups", "dp"), None),
    )
    out_specs = (
        P(("groups", "dp"), "tensor"),
        P(("groups", "dp"), "tensor"),
        P(("groups", "dp"), "tensor"),
        P(("groups", "tensor"), "dp"),
    )
    return jax.shard_map(shards, mesh=mesh, in_specs=in_specs, out_specs=out_specs, check_vma=False)
```

profile of v0, /device:TPU:0, one launch (start us, length us, event | category | flops | bytes accessed | tf_op | source)
XLA Modules:
  0.0 226.7 jit_solution(17024745603641305551)
XLA Ops:
  7.2 0.0 copy-start
  7.2 0.0 all-gather.3.cloned.1.call-start
  7.2 0.7 all-gather.3.cloned.1.call-update
  7.9 0.0 all-gather.5.cloned.1.call-start
  8.0 0.7 all-gather.5.cloned.1.call-update
  8.7 0.0 reduce-scatter.2.cloned.1.call-start
  8.7 0.8 reduce-window.8
  9.5 0.1 convert_reduce_fusion
  9.6 1.3 fusion.11
  10.9 0.2 fusion.4
  11.1 150.8 %all-gather.3.cloned.1.call-done = bf16[512,8192]{1,0:T(8,128)(2,1)} async-done(((bf16[128,8192]{1,0:T(8,128)(2,1)}), bf16[512,8192]{1,0:T(8,128)(2,1)}) %all-gather.3.cloned.1.call-update) | async-done | bytes 8388624 | tf_op jit(solution)/shard_map/all_gather | solution.py:39
  161.9 0.0 copy-done
  161.9 6.5 %convolution_convert_fusion = bf16[128,8192]{1,0:T(8,128)(2,1)} fusion(bf16[512,8192]{1,0:T(8,128)(2,1)} %all-gather.3.cloned.1.call-done, bf16[512,128]{1,0:T(8,128)(2,1)S(1)} %copy-done, f32[512,512]{0,1:T(8,128)S(1)} %get-tuple-element.13, f32[512]{0:T(512)S(1)} %fusion.4, f32[512]{0:T(512)S(1)} %get-tuple-element.12), kind=kOutput, calls=%fused_computation | convolution fusion | flops 1142751232 | bytes 11669504 | tf_op jit(solution)/shard_map/dot_general | solution.py:43
  168.4 0.0 reduce-scatter.2.cloned.1.call-update
  168.4 15.8 %all-gather.5.cloned.1.call-done = bf16[128,8192]{1,0:T(8,128)(2,1)} async-done(((bf16[128,2048]{1,0:T(8,128)(2,1)}), bf16[128,8192]{1,0:T(8,128)(2,1)}) %all-gather.5.cloned.1.call-update) | async-done | bytes 2097168 | tf_op jit(solution)/shard_map/all_gather | solution.py:38
  184.3 6.3 %convolution_convert_fusion.5 = bf16[512,128]{1,0:T(8,128)(2,1)S(1)} fusion(bf16[512,8192]{1,0:T(8,128)(2,1)} %all-gather.3.cloned.1.call-done, bf16[128,8192]{1,0:T(8,128)(2,1)} %all-gather.5.cloned.1.call-done), kind=kOutput, calls=%fused_computation.7 | convolution fusion | flops 1073807360 | bytes 10616832 | tf_op jit(solution)/shard_map/dot_general | solution.py:40
  190.6 0.3 fusion.1
  190.9 0.0 copy-start.1
  190.9 0.0 copy-start.2
  191.0 0.8 copy.11
  191.7 0.3 multiply_reduce_fusion
  192.0 0.3 multiply_convert_fusion
  192.3 0.0 copy-done.1
  192.3 1.0 convolution_convert_fusion.3
  193.3 0.0 copy-done.2
  193.3 1.0 convolution_convert_fusion.4
  194.3 23.7 %reduce-scatter.2.cloned.1.call-done = bf16[128,2048]{1,0:T(8,128)(2,1)} async-done(((bf16[128,8192]{1,0:T(8,128)(2,1)}), bf16[128,2048]{1,0:T(8,128)(2,1)}) %reduce-scatter.2.cloned.1.call-update) | async-done | bytes 524304 | tf_op jit(solution)/shard_map/reduce_scatter | solution.py:46
  218.0 2.1 convert_element_type.58
Async XLA Ops:
  7.2 154.8 %copy-start = (bf16[512,128]{1,0:T(8,128)(2,1)S(1)}, bf16[512,128]{1,0:T(8,128)(2,1)}, u32[]{:S(2)}) copy-start(bf16[512,128]{1,0:T(8,128)(2,1)} %param.8) | copy-start | bytes 393220
  7.2 154.7 %all-gather.3.cloned.1.call-start = ((), (), s32[]{:S(2)}) async-start(), calls=%async_computation.1 | async-start | bytes 10485760 | tf_op jit(solution)/shard_map/all_gather | solution.py:39
  7.9 176.4 %all-gather.5.cloned.1.call-start = ((), (), s32[]{:S(2)}) async-start(), calls=%async_computation.2 | async-start | bytes 2621440 | tf_op jit(solution)/shard_map/all_gather | solution.py:38
  8.7 209.3 %reduce-scatter.2.cloned.1.call-start = ((), (), s32[]{:S(2)}) async-start(), calls=%async_computation.3 | async-start | bytes 2621440 | tf_op jit(solution)/shard_map/reduce_scatter | solution.py:46
  190.9 1.4 copy-start.1
  190.9 2.4 %copy-start.2 = (bf16[512,128]{1,0:T(8,128)(2,1)S(1)}, bf16[512,128]{1,0:T(8,128)(2,1)}, u32[]{:S(2)}) copy-start(bf16[512,128]{1,0:T(8,128)(2,1)} %param.7) | copy-start | bytes 393220
Sparse Core Ops, SparseCore 0:
  9.6 152.3 all-gather.2
  163.5 20.7 all-gather.4
  186.8 31.1 reduce-scatter.1
where the time goes:
time: 227 us
  waiting for transfers between devices  192 us (85%)
  matrix products  16.7 us (7%)
  between operations  13.8 us (6%)
  other arithmetic  3.53 us (2%)
    all_gather x1, waiting for transfers between devices, shards(): gathered = lax.all_gather(upstream, 'tensor', axis=0, tiled=True)  151 us
    reduce_scatter x1, waiting for transfers between devices, shards(): lax.psum_scatter(partial_grad.astype(jnp.bfloat16), 'dp', scatter_dimensi...  23.7 us
    all_gather x1, waiting for transfers between devices, shards(): full_projection = lax.all_gather(projection, 'dp', axis=1, tiled=True)  15.8 us
    dot_general x1, matrix products, shards(): lax.dot_general(attended, gathered, (((0,), (0,)), ((), ())), preferred_e...  6.48 us
    dot_general x1, matrix products, shards(): lax.dot_general(gathered, full_projection, (((1,), (1,)), ((), ())), pref...  6.31 us
  transfers between devices with their start and end apart: 3, of which 3 were waited for; matrix products, arithmetic and copies ran while one was open for 8% of the time, Pallas kernels for 0%

commit v1 on v0

--- a/solution.py
+++ b/solution.py
@@ -35,7 +35,12 @@
         "hqk,khd->qhd", probs_low, value_heads, preferred_element_type=jnp.float32
     )
     attended = attended.astype(jnp.bfloat16).reshape(row_count, width)
-    full_projection = lax.all_gather(projection, "dp", axis=1, tiled=True)
+    ring = [projection]
+    for hop in range(3):
+        ring.append(lax.ppermute(ring[-1], "dp", [(dev, (dev + 1) % 4) for dev in range(4)]))
+    full_projection = jnp.roll(
+        jnp.concatenate(ring[::-1], axis=1), (lax.axis_index("dp") + 1) * ring[0].shape[1], axis=1
+    )
     gathered = lax.all_gather(upstream, "tensor", axis=0, tiled=True)
     out_total = lax.dot_general(
         gathered, full_projection, (((1,), (1,)), ((), ())), preferred_element_type=jnp.float32

time: 227 us -> 207 us (0.912)
  waiting for transfers between devices: 192 us -> 170 us
    all_gather x1 -> x0, waiting for transfers between devices: 15.8 us -> none  [shards(): full_projection = lax.all_gather(projection, 'dp', axis=1, tiled=True)]
    ppermute x0 -> x3, waiting for transfers between devices: none -> 15.1 us  [shards(): lax.ppermute(ring[-1], 'dp', [(dev, (dev + 1) % 4) for dev in range(4)])]
    all_gather x1, waiting for transfers between devices: 151 us -> 136 us  [shards(): gathered = lax.all_gather(upstream, 'tensor', axis=0, tiled=True)]
    reduce_scatter x1, waiting for transfers between devices: 23.7 us -> 17.9 us  [shards(): lax.psum_scatter(partial_grad.astype(jnp.bfloat16), 'dp', scatter_dimensi...]
  transfers between devices with their start and end apart: 3 -> 5, of which waited for: 3 -> 4; matrix products, arithmetic and copies ran while one was open for 8% -> 9% of each run, Pallas kernels for 0% -> 0%
where the time goes in v1:
time: 207 us
  waiting for transfers between devices  170 us (82%)
  matrix products  17.2 us (8%)
  between operations  14.2 us (7%)
  other arithmetic  3.51 us (2%)
    all_gather x1, waiting for transfers between devices, shards(): gathered = lax.all_gather(upstream, 'tensor', axis=0, tiled=True)  136 us
    reduce_scatter x1, waiting for transfers between devices, shards(): lax.psum_scatter(partial_grad.astype(jnp.bfloat16), 'dp', scatter_dimensi...  17.9 us
    ppermute x3, waiting for transfers between devices, shards(): lax.ppermute(ring[-1], 'dp', [(dev, (dev + 1) % 4) for dev in range(4)])  15.1 us
    dot_general x1, matrix products, shards(): lax.dot_general(gathered, full_projection, (((1,), (1,)), ((), ())), pref...  6.66 us
    dot_general x1, matrix products, shards(): lax.dot_general(attended, gathered, (((0,), (0,)), ((), ())), preferred_e...  6.57 us
  transfers between devices with their start and end apart: 5, of which 4 were waited for; matrix products, arithmetic and copies ran while one was open for 9% of the time, Pallas kernels for 0%

profile of v1, /device:TPU:0, one launch (start us, length us, event | category | flops | bytes accessed | tf_op | source)
XLA Modules:
  0.0 207.0 jit_solution(1062112834928038333)
XLA Ops:
  7.2 0.0 copy-start
  7.2 0.0 all-gather.2.cloned.1.call-start
  7.2 0.7 all-gather.2.cloned.1.call-update
  7.9 0.0 reduce-scatter.2.cloned.1.call-start
  8.0 0.5 collective-permute-start
  8.5 0.8 reduce-window.8
  9.3 8.2 %collective-permute-done = bf16[128,2048]{1,0:T(8,128)(2,1)S(1)} collective-permute-done((bf16[128,2048]{1,0:T(8,128)(2,1)}, bf16[128,2048]{1,0:T(8,128)(2,1)S(1)}, u32[]{:S(2)}, u32[]{:S(2)}) %collective-permute-start) | collective-permute-done | bytes 524320 | tf_op jit(solution)/shard_map/ppermute | solution.py:40
  17.5 0.0 collective-permute-start.1
  17.5 0.1 convert_reduce_fusion
  17.6 1.3 fusion.17
  18.9 0.2 fusion.9
  19.1 7.0 %collective-permute-done.1 = bf16[128,2048]{1,0:T(8,128)(2,1)S(1)} collective-permute-done((bf16[128,2048]{1,0:T(8,128)(2,1)S(1)}, bf16[128,2048]{1,0:T(8,128)(2,1)S(1)}, u32[]{:S(2)}, u32[]{:S(2)}) %collective-permute-start.1) | collective-permute-done | bytes 524320 | tf_op jit(solution)/shard_map/ppermute | solution.py:40
  26.1 0.0 collective-permute-start.2
  26.1 135.9 %all-gather.2.cloned.1.call-done = bf16[512,8192]{1,0:T(8,128)(2,1)} async-done(((bf16[128,8192]{1,0:T(8,128)(2,1)}), bf16[512,8192]{1,0:T(8,128)(2,1)}) %all-gather.2.cloned.1.call-update) | async-done | bytes 8388624 | tf_op jit(solution)/shard_map/all_gather | solution.py:44
  162.0 0.0 copy-done
  162.0 6.6 %convolution_convert_fusion = bf16[128,8192]{1,0:T(8,128)(2,1)} fusion(bf16[512,8192]{1,0:T(8,128)(2,1)} %all-gather.2.cloned.1.call-done, bf16[512,128]{1,0:T(8,128)(2,1)S(1)} %copy-done, f32[512,512]{0,1:T(8,128)S(1)} %get-tuple-element.13, f32[512]{0:T(512)S(1)} %fusion.9, f32[512]{0:T(512)S(1)} %get-tuple-element.12), kind=kOutput, calls=%fused_computation | convolution fusion | flops 1142751232 | bytes 11669504 | tf_op jit(solution)/shard_map/dot_general | solution.py:48
  168.5 0.0 copy-start.1
  168.5 0.0 reduce-scatter.2.cloned.1.call-update
  168.6 0.0 collective-permute-done.2
  168.7 0.8 copy-done.1
  169.8 6.7 %fusion.3 = bf16[128,512]{1,0:T(8,128)(2,1)S(1)} fusion(bf16[512,8192]{1,0:T(8,128)(2,1)} %all-gather.2.cloned.1.call-done, bf16[128,16384]{1,0:T(8,128)(2,1)S(1)} %constant_dynamic-update-slice_fusion, s32[]{:T(128)S(6)} %select_n.20), kind=kOutput, calls=%fused_computation.9 | convolution fusion | flops 1073807360 | bytes 10616836 | tf_op jit(solution)/shard_map/dot_general | solution.py:45
  176.5 0.3 fusion.6
  176.8 0.0 copy-start.2
  176.8 0.0 copy-start.3
  176.9 0.8 copy.11
  177.6 0.3 multiply_reduce_fusion
  177.9 0.3 multiply_convert_fusion
  178.2 0.0 copy-done.2
  178.2 1.0 convolution_convert_fusion.3
  179.2 0.0 copy-done.3
  179.2 1.0 convolution_convert_fusion.4
  180.2 17.9 %reduce-scatter.2.cloned.1.call-done = bf16[128,2048]{1,0:T(8,128)(2,1)} async-done(((bf16[128,8192]{1,0:T(8,128)(2,1)}), bf16[128,2048]{1,0:T(8,128)(2,1)}) %reduce-scatter.2.cloned.1.call-update) | async-done | bytes 524304 | tf_op jit(solution)/shard_map/reduce_scatter | solution.py:51
  198.1 2.1 %convert_element_type.59 = f32[128,2048]{1,0:T(8,128)} convert(bf16[128,2048]{1,0:T(8,128)(2,1)} %reduce-scatter.2.cloned.1.call-done) | non-fusion elementwise | flops 262144 | bytes 1572864 | tf_op jit(solution)/shard_map/convert_element_type | solution.py:53
  (8 shorter events, 0.3 us)
Async XLA Ops:
  7.2 154.8 %copy-start = (bf16[512,128]{1,0:T(8,128)(2,1)S(1)}, bf16[512,128]{1,0:T(8,128)(2,1)}, u32[]{:S(2)}) copy-start(bf16[512,128]{1,0:T(8,128)(2,1)} %param.8) | copy-start | bytes 393220
  7.2 154.8 %all-gather.2.cloned.1.call-start = ((), (), s32[]{:S(2)}) async-start(), calls=%async_computation.1 | async-start | bytes 10485760 | tf_op jit(solution)/shard_map/all_gather | solution.py:44
  7.9 190.2 %reduce-scatter.2.cloned.1.call-start = ((), (), s32[]{:S(2)}) async-start(), calls=%async_computation.2 | async-start | bytes 2621440 | tf_op jit(solution)/shard_map/reduce_scatter | solution.py:51
  8.0 9.5 %collective-permute-start = (bf16[128,2048]{1,0:T(8,128)(2,1)}, bf16[128,2048]{1,0:T(8,128)(2,1)S(1)}, u32[]{:S(2)}, u32[]{:S(2)}) collective-permute-start(bf16[128,2048]{1,0:T(8,128)(2,1)} %param.10), channel_id=1, source_target_pairs={{0,4},{4,8},{8,12},{12,0},{1,5},{5,9},{9,13},{13,1},{2,6},{6,10},{... | collective-permute-start | bytes 1572872 | tf_op jit(solution)/shard_map/ppermute | solution.py:40
  17.5 8.6 %collective-permute-start.1 = (bf16[128,2048]{1,0:T(8,128)(2,1)S(1)}, bf16[128,2048]{1,0:T(8,128)(2,1)S(1)}, u32[]{:S(2)}, u32[]{:S(2)}) collective-permute-start(bf16[128,2048]{1,0:T(8,128)(2,1)S(1)} %collective-permute-done), channel_id=1, source_target_pairs={{0,4},{4,8},{8,12},{12,0},{1,5},{5,9},{9,13},{13,1},{2,6},{6,10},{... | collective-permute-start | bytes 1572872 | tf_op jit(solution)/shard_map/ppermute | solution.py:40
  26.1 142.5 %collective-permute-start.2 = (bf16[128,2048]{1,0:T(8,128)(2,1)S(1)}, bf16[128,2048]{1,0:T(8,128)(2,1)S(1)}, u32[]{:S(2)}, u32[]{:S(2)}) collective-permute-start(bf16[128,2048]{1,0:T(8,128)(2,1)S(1)} %collective-permute-done.1), channel_id=1, source_target_pairs={{0,4},{4,8},{8,12},{12,0},{1,5},{5,9},{9,13},{13,1},{2,6},{6,10},{... | collective-permute-start | bytes 1572872 | tf_op jit(solution)/shard_map/ppermute | solution.py:40
  168.5 1.0 copy-start.1
  176.8 1.4 copy-start.2
  176.8 2.4 %copy-start.3 = (bf16[512,128]{1,0:T(8,128)(2,1)S(1)}, bf16[512,128]{1,0:T(8,128)(2,1)}, u32[]{:S(2)}) copy-start(bf16[512,128]{1,0:T(8,128)(2,1)} %param.7) | copy-start | bytes 393220
Sparse Core Ops, SparseCore 0:
  9.6 152.3 all-gather.1
  168.7 29.3 reduce-scatter.1
